TPU v7x, 256 devices: a whole 4x4x8 slice. The times are simulated.
256 devices in a mesh: grp: 4 (over x), dev: 64 (over y, z, core).
Axes of the slice: x: 4, y: 4, z: 8, core: 2. Of those that a mesh axis runs over, the one named last changes fastest.
Arguments:
- positions: float32 [3, 65536], P(None, ('grp', 'dev')), may hold values from -1 to 1
- velocities: float32 [3, 65536], P(None, ('grp', 'dev')), may hold values from -4 to 4
- accel_old: float32 [3, 65536], P(None, ('grp', 'dev')), may hold values from -6 to 6
- jerk_old: float32 [3, 65536], P(None, ('grp', 'dev')), may hold values from -6 to 6
- masses: float32 [65536], P(('grp', 'dev')), may hold values from 3.0517579e-06 to 7.6293945e-05
- levels: int32 [65536], P(('grp', 'dev')), may hold values from 0 to 3
- live_count: int32 [256], P(('grp', 'dev')), may hold values from 128 to 256, as said below
- active_slot: int32 [32768], P(('grp', 'dev')), may hold values from 0 to 255, as said below
Outputs:
- pos_vel: float32 [6, 32768], P(None, ('grp', 'dev'))
- acc_jerk: float32 [6, 32768], P(None, ('grp', 'dev'))
- potential: float32 [32768], P(('grp', 'dev'))
Inputs may be any that keep to these rules, and one draw needn't show every extreme that they name: `live_count`: every entry is at least 128; some device is full with 256 and some has exactly 128; the counts are uneven across devices. `active_slot`: within each device's aligned block of 128 entries the slots are distinct and below that device's live_count.
All inputs are finite; a program needn't handle non-finite values.
Results may differ from a plain program's by a relative error of at most 0.00029.
Values sent between devices are 32-bit elements; how exact they have to be, the bound alone decides.
No kernel may reach another device: no remote copies, remote signals or barrier semaphores. Data moves between devices by JAX's collectives and lax.ppermute only.
A program may use at most 64 MiB of HBM per device.

v0:
```python
import jax
import jax.numpy as jnp
from jax import lax
from jax.sharding import PartitionSpec as P

tau_base = 0.5
soften_sq = 0.0001


def pair_terms(active_state, src_pos, src_vel, src_mass):
    delta_pos = src_pos[:, None, :] - active_state[0:3, :, None]
    delta_vel = src_vel[:, None, :] - active_state[3:6, :, None]
    dist_sq = jnp.sum(delta_pos * delta_pos, axis=0) + soften_sq
    weight = src_mass[None, :] / jnp.sqrt(dist_sq)
    cubed = weight / dist_sq
    radial = 3.0 * jnp.sum(delta_pos * delta_vel, axis=0) / dist_sq
    accel = jnp.sum(cubed[None] * delta_pos, axis=2)
    jerk_new = jnp.sum(cubed[None] * (delta_vel - radial[None] * delta_pos), axis=2)
    pot_sum = -jnp.sum(weight, axis=1)
    return jnp.concatenate([accel, jerk_new, pot_sum[None]], axis=0)


def correct(state, summed):
    pos_now = state[0:3]
    vel_now = state[3:6]
    acc_start = state[6:9]
    jerk_start = state[9:12]
    step_size = state[12:13]
    acc_end = summed[0:3]
    jerk_end = summed[3:6]
    differ = acc_start - acc_end
    fourth = -6.0 * differ - step_size * (4.0 * jerk_start + 2.0 * jerk_end)
    fifth = 12.0 * differ + 6.0 * step_size * (jerk_start + jerk_end)
    new_pos = (
        pos_now + step_size * step_size / 24.0 * fourth + step_size * step_size / 120.0 * fifth
    )
    new_vel = vel_now + step_size / 6.0 * fourth + step_size / 24.0 * fifth
    return (jnp.concatenate([new_pos, new_vel], axis=0), summed[0:6], summed[6])


def sweep_sources(active_state, pos_pred, vel_pred, live_mass):
    n_active = active_state.shape[1]
    block_size = min(512, n_active)
    blocks = active_state.reshape(6, n_active // block_size, block_size).transpose(1, 0, 2)

    def one_block(block):
        return pair_terms(block, pos_pred, vel_pred, live_mass)

    partial_value = lax.map(one_block, blocks)
    return partial_value.transpose(1, 0, 2).reshape(7, n_active)


def shards(positions, velocities, accel_old, jerk_old, masses, levels, live_count, active_slot):
    elapsed = tau_base * jnp.exp2(-levels.astype(jnp.float32))
    pos_pred = positions + elapsed * (
        velocities + elapsed * (accel_old / 2.0 + elapsed * jerk_old / 6.0)
    )
    vel_pred = velocities + elapsed * (accel_old + elapsed * jerk_old / 2.0)
    slots = jnp.arange(positions.shape[1], dtype=jnp.int32)
    live_mass = jnp.where(slots < live_count[0], masses, jnp.float32(0.0))
    owned = jnp.concatenate(
        [
            pos_pred[:, active_slot],
            vel_pred[:, active_slot],
            accel_old[:, active_slot],
            jerk_old[:, active_slot],
            elapsed[active_slot][None],
        ],
        axis=0,
    )
    active = lax.all_gather(owned[0:6], ("grp", "dev"), axis=1, tiled=True)
    partial_value = sweep_sources(active, pos_pred, vel_pred, live_mass)
    summed = lax.psum_scatter(partial_value, ("grp", "dev"), scatter_dimension=1, tiled=True)
    return correct(owned, summed)


def solution(mesh):
    return jax.shard_map(
        shards,
        mesh=mesh,
        in_specs=(
            P(None, ("grp", "dev")),
            P(None, ("grp", "dev")),
            P(None, ("grp", "dev")),
            P(None, ("grp", "dev")),
            P(("grp", "dev")),
            P(("grp", "dev")),
            P(("grp", "dev")),
            P(("grp", "dev")),
        ),
        out_specs=(P(None, ("grp", "dev")), P(None, ("grp", "dev")), P(("grp", "dev"))),
        check_vma=False,
    )
```

profile of v0, /device:TPU:0, one launch (start us, length us, event | category | flops | bytes accessed | tf_op | source)
XLA Modules:
  0.0 1480.0 jit_solution(7230137608994621387)
XLA Ops:
  11.1 64.7 %all_gather.3 = f32[6,32768]{1,0:T(8,128)S(1)} all-gather(f32[6,128]{1,0:T(8,128)S(1)} %pad_maximum_fusion), channel_id=1, replica_groups=mesh['grp'=4,'dev'=64] {'grp','dev'}, dimensions={1}, use_global_device_ids=true | all-gather | bytes 789504 | tf_op jit(solution)/shard_map/all_gather | solution.py:71
  76.5 109.0 %while.10 = (s32[]{:T(128)}, f32[64,7,512]{2,1,0:T(8,128)S(1)}, f32[256]{0:T(256)S(1)}, f32[3,256]{1,0:T(4,128)S(1)}, f32[64,6,512]{2,1,0:T(8,128)S(1)}, /*index...) while((s32[]{:T(128)}, f32[64,7,512]{2,1,0:T(8,128)S(1)}, f32[256]{0:T(256)S(1)}, f32[3,256]{1,0:T(4,128)S(1)}, ...), condition=%wide.region_6.7_spmd, body=%wide.region_0.6_spmd.sunk | while | flops 6033411 | bytes 4310133 | solution.py:49
  77.3 0.9 fusion.21
  79.0 0.9 fusion.21
  80.7 0.9 fusion.21
  82.4 0.9 fusion.21
  84.1 0.9 fusion.21
  85.8 0.9 fusion.21
  87.5 0.9 fusion.21
  89.2 0.9 fusion.21
  90.9 0.9 fusion.21
  92.6 0.9 fusion.21
  94.3 0.9 fusion.21
  96.0 0.9 fusion.21
  97.7 0.9 fusion.21
  99.4 0.9 fusion.21
  101.1 0.9 fusion.21
  102.8 0.9 fusion.21
  104.5 0.9 fusion.21
  106.2 0.9 fusion.21
  107.9 0.9 fusion.21
  109.6 0.9 fusion.21
  111.3 0.9 fusion.21
  113.0 0.9 fusion.21
  114.7 0.9 fusion.21
  116.4 0.9 fusion.21
  118.1 0.9 fusion.21
  119.8 0.9 fusion.21
  121.5 0.9 fusion.21
  123.2 0.9 fusion.21
  124.9 0.9 fusion.21
  126.6 0.9 fusion.21
  128.3 0.9 fusion.21
  130.0 0.9 fusion.21
  131.8 0.9 fusion.21
  133.5 0.9 fusion.21
  135.2 0.9 fusion.21
  136.9 0.9 fusion.21
  138.6 0.9 fusion.21
  140.3 0.9 fusion.21
  142.0 0.9 fusion.21
  143.7 0.9 fusion.21
  145.4 0.9 fusion.21
  147.1 0.9 fusion.21
  148.8 0.9 fusion.21
  153.9 0.9 fusion.21
  155.6 0.9 fusion.21
  157.3 0.9 fusion.21
  159.0 0.9 fusion.21
  160.7 0.9 fusion.21
  162.4 0.9 fusion.21
  164.1 0.9 fusion.21
  165.8 0.9 fusion.21
  170.9 0.9 fusion.21
  172.6 0.9 fusion.21
  174.3 0.9 fusion.21
  176.0 0.9 fusion.21
  177.7 0.9 fusion.21
  179.4 0.9 fusion.21
  181.1 0.9 fusion.21
  185.6 1.0 copy-done
  186.5 1.3 gather_fusion.1
  189.5 1281.0 %reduce-scatter.2.cloned.1.call-done = f32[7,128]{1,0:T(8,128)} async-done(((f32[7,32768]{1,0:T(8,128)}), f32[7,128]{1,0:T(8,128)}) %reduce-scatter.2.cloned.1.call-update) | async-done | bytes 3600 | tf_op jit(solution)/shard_map/reduce_scatter | solution.py:73
  1471.9 1.2 slice_bitcast_fusion
  (358 shorter events, 59.4 us)
Async XLA Ops:
  7.2 69.3 %copy-start.3 = (f32[256]{0:T(256)S(1)}, f32[256]{0:T(256)}, u32[]{:S(2)}) copy-start(f32[256]{0:T(256)} %param.14) | copy-start | bytes 3076
  7.2 1463.4 %reduce-scatter.2.cloned.1.call-start = ((), (), s32[]{:S(2)}) async-start(), calls=%async_computation.1 | async-start | bytes 1052672 | tf_op jit(solution)/shard_map/reduce_scatter | solution.py:73
  185.5 1.0 copy-start
  185.5 2.3 copy-start.1
  185.5 2.4 copy-start.2
Sparse Core Ops, SparseCore 0:
  186.7 1283.8 reduce-scatter.1
where the time goes:
time: 1480 us
  waiting for transfers between devices  1280 us (86%)
  other arithmetic  109 us (7%)
  blocking collectives  64.7 us (4%)
  between operations  14.8 us (1%)
    reduce_scatter x1, waiting for transfers between devices, shards(): lax.psum_scatter(partial_value, ('grp', 'dev'), scatter_dimension=1, tile...  1280 us
    all_gather x1, blocking collectives, shards(): active = lax.all_gather(owned[0:6], ('grp', 'dev'), axis=1, tiled=True)  64.7 us
    reduce_sum x64, other arithmetic, pair_terms(): accel = jnp.sum(cubed[None] * delta_pos, axis=2)  59.3 us
    reduce_sum x64, other arithmetic, pair_terms(): radial = 3.0 * jnp.sum(delta_pos * delta_vel, axis=0) / dist_sq  30.3 us
  transfers between devices with their start and end apart: 1, of which 1 were waited for; matrix products, arithmetic and copies ran while one was open for 0% of the time, Pallas kernels for 0%

commit v1 on v0

--- a/solution.py
+++ b/solution.py
@@ -68,7 +68,9 @@
         ],
         axis=0,
     )
-    active = lax.all_gather(owned[0:6], ("grp", "dev"), axis=1, tiled=True)
+    part = owned[0:6]
+    sent = jnp.stack([part] * lax.axis_size(("grp", "dev")))
+    active = jnp.concatenate(lax.all_to_all(sent, ("grp", "dev"), 0, 0), axis=1)
     partial_value = sweep_sources(active, pos_pred, vel_pred, live_mass)
     summed = lax.psum_scatter(partial_value, ("grp", "dev"), scatter_dimension=1, tiled=True)
     return correct(owned, summed)

time: 1480 us -> 1460 us (0.986)
  blocking collectives: 64.7 us -> 0 us
  waiting for transfers between devices: 1280 us -> 1310 us
    all_gather x1 -> x0, blocking collectives: 64.7 us -> none  [shards(): active = lax.all_gather(owned[0:6], ('grp', 'dev'), axis=1, tiled=True)]
    all_to_all x0 -> x1, waiting for transfers between devices: none -> 28.4 us  [shards(): active = jnp.concatenate(lax.all_to_all(sent, ('grp', 'dev'), 0, 0), axis=1)]
  transfers between devices with their start and end apart: 1 -> 2, of which waited for: 1 -> 2; matrix products, arithmetic and copies ran while one was open for 0% -> 0% of each run, Pallas kernels for 0% -> 0%
where the time goes in v1:
time: 1460 us
  waiting for transfers between devices  1310 us (90%)
  other arithmetic  109 us (7%)
  between operations  14.8 us (1%)
  starting transfers between devices  14.6 us (1%)
    reduce_scatter x1, waiting for transfers between devices, shards(): lax.psum_scatter(partial_value, ('grp', 'dev'), scatter_dimension=1, tile...  1280 us
    reduce_sum x64, other arithmetic, pair_terms(): accel = jnp.sum(cubed[None] * delta_pos, axis=2)  59.3 us
    reduce_sum x64, other arithmetic, pair_terms(): radial = 3.0 * jnp.sum(delta_pos * delta_vel, axis=0) / dist_sq  30.3 us
  transfers between devices with their start and end apart: 2, of which 2 were waited for; matrix products, arithmetic and copies ran while one was open for 0% of the time, Pallas kernels for 0%

profile of v1, /device:TPU:0, one launch (start us, length us, event | category | flops | bytes accessed | tf_op | source)
XLA Modules:
  0.0 1457.7 jit_solution(2480056466963752788)
XLA Ops:
  11.0 1.1 stack.2
  12.1 14.6 %all-to-all-start = ((f32[256,6,128]{2,1,0:T(8,128)}), f32[256,6,128]{2,1,0:T(8,128)S(1)}, u32[]{:S(2)}, u32[]{:S(2)}) async-start(f32[256,6,128]{2,1,0:T(8,128)} %stack.2), calls=%async_computation | async-start | bytes 2097152 | tf_op jit(solution)/shard_map/all_to_all | solution.py:73
  27.4 28.4 %all-to-all-done = f32[256,6,128]{2,1,0:T(8,128)S(1)} async-done(((f32[256,6,128]{2,1,0:T(8,128)}), f32[256,6,128]{2,1,0:T(8,128)S(1)}, u32[]{:S(2)}, u32[]{:S(2)}) %all-to-all-start) | async-done | bytes 786464 | tf_op jit(solution)/shard_map/all_to_all | solution.py:73
  55.8 108.8 %while.10 = (s32[]{:T(128)}, f32[64,7,512]{2,1,0:T(8,128)S(1)}, f32[256]{0:T(256)S(1)}, f32[3,256]{1,0:T(4,128)S(1)}, f32[64,6,512]{2,1,0:T(8,128)S(1)}, /*index...) while((s32[]{:T(128)}, f32[64,7,512]{2,1,0:T(8,128)S(1)}, f32[256]{0:T(256)S(1)}, f32[3,256]{1,0:T(4,128)S(1)}, ...), condition=%wide.region_6.7_spmd, body=%wide.region_0.6_spmd.sunk | while | flops 6033411 | bytes 4310133 | solution.py:49
  56.6 0.9 fusion.21
  58.3 0.9 fusion.21
  60.0 0.9 fusion.21
  61.7 0.9 fusion.21
  63.4 0.9 fusion.21
  65.1 0.9 fusion.21
  66.8 0.9 fusion.21
  68.5 0.9 fusion.21
  70.2 0.9 fusion.21
  71.9 0.9 fusion.21
  73.6 0.9 fusion.21
  75.3 0.9 fusion.21
  77.0 0.9 fusion.21
  78.7 0.9 fusion.21
  80.4 0.9 fusion.21
  82.1 0.9 fusion.21
  83.8 0.9 fusion.21
  85.5 0.9 fusion.21
  87.2 0.9 fusion.21
  88.9 0.9 fusion.21
  90.6 0.9 fusion.21
  92.3 0.9 fusion.21
  94.0 0.9 fusion.21
  95.7 0.9 fusion.21
  97.4 0.9 fusion.21
  99.1 0.9 fusion.21
  100.8 0.9 fusion.21
  102.5 0.9 fusion.21
  104.2 0.9 fusion.21
  105.9 0.9 fusion.21
  107.6 0.9 fusion.21
  109.3 0.9 fusion.21
  111.0 0.9 fusion.21
  112.7 0.9 fusion.21
  114.4 0.9 fusion.21
  117.8 0.9 fusion.21
  119.5 0.9 fusion.21
  122.9 0.9 fusion.21
  124.6 0.9 fusion.21
  128.0 0.9 fusion.21
  129.7 0.9 fusion.21
  133.1 0.9 fusion.21
  134.8 0.9 fusion.21
  136.5 0.9 fusion.21
  138.2 0.9 fusion.21
  139.9 0.9 fusion.21
  141.6 0.9 fusion.21
  143.3 0.9 fusion.21
  145.0 0.9 fusion.21
  146.7 0.9 fusion.21
  150.1 0.9 fusion.21
  151.8 0.9 fusion.21
  155.2 0.9 fusion.21
  156.9 0.9 fusion.21
  160.3 0.9 fusion.21
  162.0 0.9 fusion.21
  164.7 1.0 copy-done
  165.7 1.3 gather_fusion.1
  168.7 1279.6 %reduce-scatter.2.cloned.1.call-done = f32[7,128]{1,0:T(8,128)} async-done(((f32[7,32768]{1,0:T(8,128)}), f32[7,128]{1,0:T(8,128)}) %reduce-scatter.2.cloned.1.call-update) | async-done | bytes 3600 | tf_op jit(solution)/shard_map/reduce_scatter | solution.py:75
  1449.7 1.2 slice_bitcast_fusion
  (360 shorter events, 61.1 us)
Async XLA Ops:
  12.1 15.3 %copy-start.3 = (f32[256]{0:T(256)S(1)}, f32[256]{0:T(256)}, u32[]{:S(2)}) copy-start(f32[256]{0:T(256)} %param.14) | copy-start | bytes 3076
  12.1 43.7 %all-to-all-start = ((f32[256,6,128]{2,1,0:T(8,128)}), f32[256,6,128]{2,1,0:T(8,128)S(1)}, u32[]{:S(2)}, u32[]{:S(2)}) async-start(f32[256,6,128]{2,1,0:T(8,128)} %stack.2), calls=%async_computation | async-start | bytes 2097152 | tf_op jit(solution)/shard_map/all_to_all | solution.py:73
  26.7 1421.6 %reduce-scatter.2.cloned.1.call-start = ((), (), s32[]{:S(2)}) async-start(), calls=%async_computation.2 | async-start | bytes 1052672 | tf_op jit(solution)/shard_map/reduce_scatter | solution.py:75
  164.7 1.0 copy-start
  164.7 2.3 copy-start.1
  164.7 2.4 copy-start.2
Sparse Core Ops, SparseCore 0:
  165.8 1282.4 reduce-scatter.1
